TPU v7x, 1024 devices: a whole 4x8x16 slice. The times are simulated.
1024 devices in a mesh: space: 64 (over x, z_lo, core), var: 16 (over y, z_hi).
Axes of the slice: x: 4, y: 8, z: 16 (z_hi: 2, z_lo: 8; z = z_hi * 8 + z_lo), core: 2. Of those that a mesh axis runs over, the one named last changes fastest.
Arguments:
- var_tokens: bfloat16 [64, 8192, 1024], P('var', 'space'), may hold values from -6 to 6
- key_query: bfloat16 [1024, 16], replicated
- value_weight: bfloat16 [1024, 1024], replicated, may hold values from -0.1875 to 0.1875
- qkv_weight: bfloat16 [1024, 3, 1024], P(None, None, 'var')
- out_weight: bfloat16 [1024, 1024], P('var'), may hold values from -0.1875 to 0.1875
- up_weight: bfloat16 [1024, 4096], P(None, 'var'), may hold values from -0.1875 to 0.1875
- down_weight: bfloat16 [4096, 1024], P('var'), may hold values from -0.09375 to 0.09375
- norm_gain: bfloat16 [1024], replicated, may hold values from 0.25 to 1.75
Outputs:
- block_out: bfloat16 [8192, 1024], P(('space', 'var'))
All inputs are finite; a program needn't handle non-finite values.
Results may differ from a plain program's by a relative error of at most 0.018.
Values may be sent and summed in bfloat16 or wider, within the bound.
A program may use at most 32 MiB of HBM per device.

v0:
```python
import jax
import jax.numpy as jnp
from jax import lax
from jax.sharding import PartitionSpec as P

H = 16


def per_device(
    var_tokens, key_query, value_weight, qkv_weight, out_weight, up_weight, down_weight, norm_gain
):
    f32 = jnp.float32
    bf16 = jnp.bfloat16
    groups = lax.axis_size("var")
    local_vars, seq_rows, feat_width = var_tokens.shape
    head_dim = feat_width // H
    local_heads = H // groups
    scores = jnp.einsum("vsd,dh->vsh", var_tokens, key_query, preferred_element_type=f32)
    values = jnp.einsum("vsd,de->vse", var_tokens, value_weight, preferred_element_type=f32).astype(
        bf16
    )
    values = values.reshape(local_vars, seq_rows, H, head_dim)
    head_values = lax.all_to_all(values, "var", split_axis=2, concat_axis=0, tiled=True)
    head_scores = lax.all_to_all(scores, "var", split_axis=2, concat_axis=0, tiled=True)
    top_score = jnp.max(head_scores, axis=0)
    exp_terms = jnp.exp(head_scores - top_score[None])
    weight_sum = jnp.sum(exp_terms, axis=0)
    numerator = jnp.einsum(
        "vsh,vshe->she", exp_terms.astype(bf16), head_values, preferred_element_type=f32
    )
    pooled = (
        (numerator / weight_sum[..., None]).reshape(seq_rows, local_heads * head_dim).astype(bf16)
    )
    all_features = lax.all_gather(pooled, "var", axis=1, tiled=True)
    pooled_f = all_features.astype(f32)
    mean_row = jnp.mean(pooled_f, axis=1, keepdims=True)
    centered = pooled_f - mean_row
    spread = jnp.mean(centered * centered, axis=1, keepdims=True)
    normed = (centered * lax.rsqrt(spread + 1e-05) * norm_gain.astype(f32)).astype(bf16)
    qkv = jnp.einsum("sd,dcj->scj", normed, qkv_weight, preferred_element_type=f32).astype(bf16)
    query_rows = qkv[:, 0].reshape(seq_rows, local_heads, head_dim)
    key_local = qkv[:, 1]
    value_local = qkv[:, 2]
    scale_attn = head_dim ** (-0.5)
    run_max = jnp.full((local_heads, seq_rows), -jnp.inf, f32)
    run_sum = jnp.zeros((local_heads, seq_rows), f32)
    run_acc = jnp.zeros((local_heads, seq_rows, head_dim), f32)
    key_block = lax.all_gather(key_local, "space", axis=0, tiled=True)
    value_block = lax.all_gather(value_local, "space", axis=0, tiled=True)
    key_rows = key_block.reshape(-1, local_heads, head_dim)
    value_rows = value_block.reshape(-1, local_heads, head_dim)
    logits = (
        jnp.einsum("shd,rhd->hsr", query_rows, key_rows, preferred_element_type=f32) * scale_attn
    )
    new_max = jnp.max(logits, axis=2)
    rescale = jnp.exp(run_max - new_max)
    exp_terms = jnp.exp(logits - new_max[..., None])
    new_sum = run_sum * rescale + jnp.sum(exp_terms, axis=2)
    update = jnp.einsum(
        "hsr,rhd->hsd", exp_terms.astype(bf16), value_rows, preferred_element_type=f32
    )
    final_acc = run_acc * rescale[..., None] + update
    attended = (
        (final_acc / new_sum[..., None])
        .transpose(1, 0, 2)
        .reshape(seq_rows, local_heads * head_dim)
        .astype(bf16)
    )
    hidden = jax.nn.gelu(
        jnp.dot(normed, up_weight, preferred_element_type=f32), approximate=True
    ).astype(bf16)
    rows_out = seq_rows // groups
    summed = lax.psum_scatter(
        (
            jnp.dot(attended, out_weight, preferred_element_type=f32)
            + jnp.dot(hidden, down_weight, preferred_element_type=f32)
        ).astype(jnp.bfloat16),
        "var",
        scatter_dimension=0,
        tiled=True,
    ).astype(jnp.float32)
    residual_rows = lax.dynamic_slice_in_dim(
        pooled_f, lax.axis_index("var") * rows_out, rows_out, 0
    )
    return (summed + residual_rows).astype(bf16)


def solution(mesh):
    placed = (
        P("var", "space", None),
        P(),
        P(),
        P(None, None, "var"),
        P("var", None),
        P(None, "var"),
        P("var", None),
        P(),
    )
    return jax.shard_map(
        per_device, mesh=mesh, in_specs=placed, out_specs=P(("space", "var"), None), check_vma=False
    )
```

profile of v0, /device:TPU:1, one launch (start us, length us, event | category | flops | bytes accessed | tf_op | source)
XLA Modules:
  0.0 712.0 jit_solution(13112444663013537706)
XLA Ops:
  6.5 0.0 copy-start
  6.5 1.7 fusion.41
  8.3 0.6 copy.12
  8.9 24.6 %all-to-all-start = ((f32[4,128,16]{1,0,2:T(4,128)}), f32[4,128,16]{1,0,2:T(4,128)S(1)}, u32[]{:S(2)}, u32[]{:S(2)}) async-start(f32[4,128,16]{1,0,2:T(4,128)} %copy.12), calls=%async_computation | async-start | bytes 65536 | tf_op jit(solution)/shard_map/all_to_all | solution.py:24
  33.6 0.0 copy-done
  33.6 3.5 fusion.7
  37.0 0.0 copy-start.3
  37.0 1.6 copy.13
  38.7 1.1 copy.14
  39.8 10.0 %all-to-all-done = f32[4,128,16]{1,0,2:T(4,128)S(1)} async-done(((f32[4,128,16]{1,0,2:T(4,128)}), f32[4,128,16]{1,0,2:T(4,128)S(1)}, u32[]{:S(2)}, u32[]{:S(2)}) %all-to-all-start) | async-done | bytes 32800 | tf_op jit(solution)/shard_map/all_to_all | solution.py:24
  49.8 6.3 all-to-all-start.1
  56.0 0.0 all-gather.5.cloned.1.call-start
  56.1 0.0 copy-done.3
  56.2 28.5 %all-to-all-done.1 = bf16[4,128,16,64]{1,3,0,2:T(8,128)(2,1)S(1)} async-done(((bf16[4,128,16,64]{1,3,0,2:T(8,128)(2,1)}), bf16[4,128,16,64]{1,3,0,2:T(8,128)(2,1)S(1)}, u32[]{:S(2)}, u32[]{:S(2)}) %all-to-all-start.1) | async-done | bytes 1048608 | tf_op jit(solution)/shard_map/all_to_all | solution.py:23
  84.7 0.3 multiply_reduce_fusion
  85.0 115.3 %all_gather.9 = bf16[128,1024]{0,1:T(8,128)(2,1)S(1)} all-gather(bf16[128,64]{0,1:T(8,128)(2,1)S(1)} %divide_convert_fusion), channel_id=1, replica_groups=mesh['space'=64,'var'=16] {'var'}, dimensions={1}, use_global_device_ids=true | all-gather | bytes 278528 | tf_op jit(solution)/shard_map/all_gather | solution.py:34
  200.3 0.1 copy.15
  200.5 0.1 convert_reduce_fusion
  200.6 0.2 multiply_reduce_fusion.1
  200.8 1.4 fusion.53
  202.2 0.6 fusion.54
  202.8 0.0 all-gather.5.cloned.1.call-update
  202.8 0.0 all-gather.7.cloned.1.call-start
  202.9 0.7 all-gather.7.cloned.1.call-update
  203.6 0.0 reduce-scatter.2.cloned.1.call-start
  203.6 1.8 fusion.33
  205.4 0.0 copy-start.2
  205.4 131.1 %all-gather.5.cloned.1.call-done = bf16[8192,1,64]{0,2,1:T(8,128)(2,1)} async-done(((bf16[128,1,64]{0,2,1:T(8,128)(2,1)}), bf16[8192,1,64]{0,2,1:T(8,128)(2,1)}) %all-gather.5.cloned.1.call-update) | async-done | bytes 1048592 | tf_op jit(solution)/shard_map/all_gather | solution.py:48
  336.5 2.0 fusion.55
  338.5 0.0 copy-start.1
  338.6 1.9 copy-done.1
  340.5 0.8 fusion
  341.2 112.7 %all-gather.7.cloned.1.call-done = bf16[8192,1,64]{0,2,1:T(8,128)(2,1)} async-done(((bf16[128,1,64]{0,2,1:T(8,128)(2,1)}), bf16[8192,1,64]{0,2,1:T(8,128)(2,1)}) %all-gather.7.cloned.1.call-update) | async-done | bytes 1048592 | tf_op jit(solution)/shard_map/all_gather | solution.py:49
  453.9 0.0 copy-done.2
  453.9 4.4 fusion.10
  458.3 0.0 reduce-scatter.2.cloned.1.call-update
  458.4 245.7 %reduce-scatter.2.cloned.1.call-done = bf16[8,1024]{1,0:T(8,128)(2,1)} async-done(((bf16[128,1024]{1,0:T(8,128)(2,1)}), bf16[8,1024]{1,0:T(8,128)(2,1)}) %reduce-scatter.2.cloned.1.call-update) | async-done | bytes 16400 | tf_op jit(solution)/shard_map/reduce_scatter | solution.py:73
  704.1 1.3 add_convert_fusion
  (10 shorter events, 0.2 us)
Async XLA Ops:
  6.5 27.0 %copy-start = (bf16[1024,1024]{1,0:T(8,128)(2,1)S(1)}, bf16[1024,1024]{1,0:T(8,128)(2,1)}, u32[]{:S(2)}) copy-start(bf16[1024,1024]{1,0:T(8,128)(2,1)} %param.10) | copy-start | bytes 6291460
  8.9 40.8 %all-to-all-start = ((f32[4,128,16]{1,0,2:T(4,128)}), f32[4,128,16]{1,0,2:T(4,128)S(1)}, u32[]{:S(2)}, u32[]{:S(2)}) async-start(f32[4,128,16]{1,0,2:T(4,128)} %copy.12), calls=%async_computation | async-start | bytes 65536 | tf_op jit(solution)/shard_map/all_to_all | solution.py:24
  37.0 19.0 %copy-start.3 = (bf16[1024]{0:T(1024)(128)(2,1)S(1)}, bf16[1024]{0:T(1024)(128)(2,1)}, u32[]{:S(2)}) copy-start(bf16[1024]{0:T(1024)(128)(2,1)} %param.15) | copy-start | bytes 6148
  49.8 34.9 %all-to-all-start.1 = ((bf16[4,128,16,64]{1,3,0,2:T(8,128)(2,1)}), bf16[4,128,16,64]{1,3,0,2:T(8,128)(2,1)S(1)}, u32[]{:S(2)}, u32[]{:S(2)}) async-start(bf16[4,128,16,64]{1,3,0,2:T(8,128)(2,1)} %copy.14), calls=%async_computation.1 | async-start | bytes 2097152 | tf_op jit(solution)/shard_map/all_to_all | solution.py:23
  56.0 280.5 %all-gather.5.cloned.1.call-start = ((), (), s32[]{:S(2)}) async-start(), calls=%async_computation.4 | async-start | bytes 1064960 | tf_op jit(solution)/shard_map/all_gather | solution.py:48
  202.8 251.1 %all-gather.7.cloned.1.call-start = ((), (), s32[]{:S(2)}) async-start(), calls=%async_computation.5 | async-start | bytes 1064960 | tf_op jit(solution)/shard_map/all_gather | solution.py:49
  203.6 500.5 %reduce-scatter.2.cloned.1.call-start = ((), (), s32[]{:S(2)}) async-start(), calls=%async_computation.3 | async-start | bytes 278528 | tf_op jit(solution)/shard_map/reduce_scatter | solution.py:73
  205.4 248.5 %copy-start.2 = (bf16[64,1024]{1,0:T(8,128)(2,1)S(1)}, bf16[64,1024]{1,0:T(8,128)(2,1)}, u32[]{:S(2)}) copy-start(bf16[64,1024]{1,0:T(8,128)(2,1)} %param.12) | copy-start | bytes 393220
  338.5 1.9 copy-start.1
Sparse Core Ops, SparseCore 0:
  203.0 133.4 all-gather.4
  339.1 114.7 all-gather.6
  459.5 244.5 reduce-scatter.1
where the time goes:
time: 717 us; the launch traced here: 712 us
  waiting for transfers between devices  529 us (74%)
  blocking collectives  115 us (16%)
  starting transfers between devices  31 us (4%)
  matrix products  14.7 us (2%)
  between operations  13.2 us (2%)
    reduce_scatter x1, waiting for transfers between devices, per_device(): lax.psum_scatter((jnp.dot(attended, out_weight, preferred_element_type=f3...  246 us
    all_gather x1, waiting for transfers between devices, per_device(): key_block = lax.all_gather(key_local, 'space', axis=0, tiled=True)  131 us
    all_gather x1, blocking collectives, per_device(): all_features = lax.all_gather(pooled, 'var', axis=1, tiled=True)  115 us
    all_gather x1, waiting for transfers between devices, per_device(): value_block = lax.all_gather(value_local, 'space', axis=0, tiled=True)  113 us
    all_to_all x1, waiting for transfers between devices, per_device(): lax.all_to_all(values, 'var', split_axis=2, concat_axis=0, tiled=True)  28.5 us
    all_to_all x1, starting transfers between devices, per_device(): lax.all_to_all(scores, 'var', split_axis=2, concat_axis=0, tiled=True)  24.6 us
  transfers between devices with their start and end apart: 5, of which 5 were waited for; matrix products, arithmetic and copies ran while one was open for 2% of the time, Pallas kernels for 0%

commit v1 on v0

v1 whole, which is shorter than its diff:
```python
import functools

import jax
import jax.numpy as jnp
from jax import lax
from jax.experimental import pallas as pl
from jax.experimental.pallas import tpu as pltpu
from jax.sharding import PartitionSpec as P

MESH = pl.DeviceIdType.MESH
F32 = jnp.float32
BF16 = jnp.bfloat16
HEAD = 64
NZH = 2
NZ = 8
NCORE = 2


def _dot(a, b, dims=(((1,), (0,)), ((), ()))):
    return lax.dot_general(a, b, dims, preferred_element_type=F32)


def _expander(heads, width):
    row = lax.broadcasted_iota(jnp.int32, (heads, width), 0)
    col = lax.broadcasted_iota(jnp.int32, (heads, width), 1)
    return jnp.where(col // HEAD == row, 1.0, 0.0).astype(BF16)


def _merge(outs, lses, spread):
    top = functools.reduce(jnp.maximum, lses)
    weights = [jnp.exp(lse - top) for lse in lses]
    total = functools.reduce(jnp.add, weights)
    shares = [w / total for w in weights]
    high = [s.astype(BF16) for s in shares]
    low = [(s - h.astype(F32)).astype(BF16) for s, h in zip(shares, high)]
    wide = _dot(jnp.concatenate(high + low, axis=0), spread)
    n, rows = len(outs), outs[0].shape[0]
    merged = None
    for k, out in enumerate(outs):
        share = wide[k * rows : (k + 1) * rows] + wide[(n + k) * rows : (n + k + 1) * rows]
        term = share * out.astype(F32)
        merged = term if merged is None else merged + term
    return merged, top + jnp.log(total)


def kernel(
    ny, ni, n_vars,
    tok_hbm, kq_ref, vw_hbm, qkv_hbm, ow_hbm, up_hbm, dw_hbm, gain_ref,
    out_ref,
    tok, vw, qkvw, ow, up, dw,
    part, stat, rpart, rstat, zpart, zstat, pooled, nbuf, kvbuf, qbuf, mlp,
    obuf, ostat, robuf, rostat, fbuf, rf, zsum, zrecv,
    load_sem, a_send, a_recv, as_send, as_recv, z_send, z_recv, n_send, n_recv,
    k_send, k_recv, q_send, q_recv, o_send, o_recv, os_send, os_recv, f_send, f_recv,
):
    rows = tok.shape[0] // n_vars
    width = tok.shape[1]
    heads = width // HEAD
    band = rows // ny

    space = lax.axis_index("space")
    var = lax.axis_index("var")
    y, zh = var // NZH, lax.rem(var, NZH)
    z = lax.rem(space // NCORE, NZ)
    i = (space // (NCORE * NZ)) * NCORE + lax.rem(space, NCORE)

    def at_y(d):
        return {"space": space, "var": lax.rem(y + d + ny, ny) * NZH + zh}

    def at_zh():
        return {"space": space, "var": y * NZH + (1 - zh)}

    def at_z(d):
        other = lax.rem(z + d, NZ)
        return {
            "space": (i // NCORE) * (NCORE * NZ) + other * NCORE + lax.rem(i, NCORE),
            "var": var,
        }

    def at_i(d):
        other = lax.rem(i + d + ni, ni)
        return {
            "space": (other // NCORE) * (NCORE * NZ) + z * NCORE + lax.rem(other, NCORE),
            "var": var,
        }

    def remote(src, dst, send, recv, peer):
        return pltpu.make_async_remote_copy(
            src_ref=src, dst_ref=dst, send_sem=send, recv_sem=recv,
            device_id=peer, device_id_type=MESH,
        )

    def far_first(n):
        return sorted(range(1, n), key=lambda d: -min(d, n - d))

    loads = [
        pltpu.make_async_copy(src, dst, load_sem.at[k])
        for k, (src, dst) in enumerate(
            [(tok_hbm, tok), (vw_hbm, vw), (qkv_hbm, qkvw), (up_hbm, up), (dw_hbm, dw), (ow_hbm, ow)]
        )
    ]
    for load in loads:
        load.start()

    barrier = pltpu.get_barrier_semaphore()
    greeted = 0
    for peers in (
        [at_y(d) for d in range(1, ny)], [at_zh()],
        [at_z(d) for d in range(1, NZ)], [at_i(d) for d in range(1, ni)],
    ):
        for peer in peers:
            pl.semaphore_signal(barrier, inc=1, device_id=peer, device_id_type=MESH)
            greeted += 1

    spread = _expander(heads, width)
    stat[...] = jnp.zeros_like(stat)
    zstat[0] = jnp.zeros_like(zstat[0])
    loads[0].wait()
    scores = _dot(tok[...], kq_ref[...])
    per_var = [scores[v * rows : (v + 1) * rows] for v in range(n_vars)]
    top = functools.reduce(jnp.maximum, per_var)
    exps = [jnp.exp(s - top) for s in per_var]
    total = functools.reduce(jnp.add, exps)
    stat[:, :heads] = top + jnp.log(total)
    shares = jnp.concatenate([(e / total).astype(BF16) for e in exps], axis=0)
    loads[1].wait()
    tile = min(256, width)
    for c in range(0, width, tile):
        values = _dot(tok[...], vw[:, c : c + tile]).astype(BF16).astype(F32)
        weighted = values * _dot(shares, spread[:, c : c + tile])
        acc = weighted[:rows]
        for v in range(1, n_vars):
            acc = acc + weighted[v * rows : (v + 1) * rows]
        part[:, c : c + tile] = acc.astype(BF16)

    pl.semaphore_wait(barrier, greeted)

    copies = []
    for d in far_first(ny):
        theirs = pl.ds(pl.multiple_of(lax.rem(y + d, ny) * band, band), band)
        for src, dst, send, recv in (
            (part, rpart, a_send, a_recv), (stat, rstat, as_send, as_recv)
        ):
            copy = remote(src.at[theirs], dst.at[d], send.at[d], recv.at[d], at_y(d))
            copy.start()
            copies.append(copy)
    for copy in copies:
        copy.wait()
    mine = pl.ds(pl.multiple_of(y * band, band), band)
    merged, lse = _merge(
        [part[mine, :]] + [rpart[d] for d in range(1, ny)],
        [stat[mine, :][:, :heads]] + [rstat[d][:, :heads] for d in range(1, ny)],
        spread,
    )

    zpart[0] = merged.astype(BF16)
    zstat[0, :, :heads] = lse
    copies = [
        remote(buf.at[0], buf.at[1], z_send.at[k], z_recv.at[k], at_zh())
        for k, buf in enumerate((zpart, zstat))
    ]
    for copy in copies:
        copy.start()
    for copy in copies:
        copy.wait()
    merged, _ = _merge(
        [zpart[0], zpart[1]], [zstat[0][:, :heads], zstat[1][:, :heads]], spread
    )
    rounded = merged.astype(BF16).astype(F32)
    pooled[...] = rounded
    centred = rounded - jnp.mean(rounded, axis=1, keepdims=True)
    spread_sq = jnp.mean(centred * centred, axis=1, keepdims=True)
    nbuf[0] = (centred * lax.rsqrt(spread_sq + 1e-05) * gain_ref[...].astype(F32)).astype(BF16)

    copies = []
    for d in far_first(ny):
        copy = remote(nbuf.at[0], nbuf.at[d], n_send.at[d], n_recv.at[d], at_y(d))
        copy.start()
        copies.append(copy)
    for copy in copies:
        copy.wait()
    normed = nbuf[...].reshape(rows, width)

    for load in loads[2:]:
        load.wait()
    qkv = _dot(normed, qkvw[...])
    kvbuf[0] = qkv[:, : 2 * HEAD].astype(BF16)
    qbuf[0] = (qkv[:, 2 * HEAD :] * HEAD**-0.5).astype(BF16)
    copies = []
    for d in range(NZ - 1, 0, -1):
        copy = remote(kvbuf.at[0], kvbuf.at[d], k_send.at[d], k_recv.at[d], at_z(d))
        copy.start()
        copies.append(copy)
    for d in far_first(ni):
        copy = remote(qbuf.at[0], qbuf.at[d], q_send.at[d], q_recv.at[d], at_i(d))
        copy.start()
        copies.append(copy)

    hidden = jax.nn.gelu(_dot(normed, up[...]), approximate=True).astype(BF16)
    mlp[...] = _dot(hidden, dw[...])
    for copy in copies:
        copy.wait()

    keys = NZ * rows
    kv = kvbuf[...].reshape(keys, 2 * HEAD)
    values_t = kv.T[HEAD:]

    def attend(d):
        logits = _dot(kv, qbuf[d], (((1,), (1,)), ((), ())))
        top = jnp.max(logits, axis=0, keepdims=True)
        exps = jnp.exp(logits - top)
        total = jnp.sum(exps, axis=0, keepdims=True)
        obuf[d] = (_dot(values_t, exps.astype(BF16)) / total).astype(BF16)
        ostat[d] = jnp.broadcast_to(top + jnp.log(total), (8, rows))

    def give(d):
        owner = at_i(-d)
        return (
            remote(obuf.at[d], robuf.at[d], o_send.at[d], o_recv.at[d], owner),
            remote(ostat.at[d], rostat.at[d], os_send.at[d], os_recv.at[d], owner),
        )

    @pl.loop(1, ni)
    def _(d):
        attend(d)
        for copy in give(d):
            copy.start()

    attend(0)
    for d in range(1, ni):
        for copy in give(d):
            copy.wait()
    lses = [ostat[0][:1]] + [rostat[d][:1] for d in range(1, ni)]
    top = functools.reduce(jnp.maximum, lses)
    weights = [jnp.exp(lse - top) for lse in lses]
    total = functools.reduce(jnp.add, weights)
    attended = obuf[0].astype(F32) * (weights[0] / total)
    for d in range(1, ni):
        attended = attended + robuf[d].astype(F32) * (weights[d] / total)

    term = _dot(attended.T.astype(BF16), ow[...]) + mlp[...]
    fbuf[...] = term.reshape(ny, band, width).astype(BF16)
    copies = []
    for d in far_first(ny):
        copy = remote(fbuf.at[d], rf.at[d], f_send.at[d], f_recv.at[d], at_y(-d))
        copy.start()
        copies.append(copy)
    for copy in copies:
        copy.wait()
    summed = term[:band]
    for d in range(1, ny):
        summed = summed + rf[d].astype(F32)
    zsum[...] = summed
    half = band // NZH
    own = pl.ds(pl.multiple_of(zh * half, half), half)
    other = pl.ds(pl.multiple_of((1 - zh) * half, half), half)
    last = remote(zsum.at[other], zrecv, z_send.at[2], z_recv.at[2], at_zh())
    last.start()
    last.wait()
    out_ref[...] = (pooled[own, :] + (zsum[own, :] + zrecv[...])).astype(BF16)


def per_device(var_tokens, key_query, value_weight, qkv_weight, out_weight, up_weight, down_weight, norm_gain):
    n_vars, rows, width = var_tokens.shape
    ny = lax.axis_size("var") // NZH
    ni = lax.axis_size("space") // NZ
    band = rows // ny
    hidden = up_weight.shape[1]
    blank = jnp.zeros((width, HEAD), BF16)
    qkv_cols = jnp.concatenate(
        [qkv_weight[:, 1], qkv_weight[:, 2], qkv_weight[:, 0], blank], axis=1
    )
    any_spec = pl.BlockSpec(memory_space=pl.ANY)
    vmem_spec = pl.BlockSpec(memory_space=pltpu.VMEM)
    dma = pltpu.SemaphoreType.DMA
    vm = pltpu.VMEM
    return pl.pallas_call(
        functools.partial(kernel, ny, ni, n_vars),
        out_shape=jax.ShapeDtypeStruct((band // NZH, width), BF16),
        in_specs=[any_spec, vmem_spec, any_spec, any_spec, any_spec, any_spec, any_spec, vmem_spec],
        out_specs=vmem_spec,
        scratch_shapes=[
            vm((n_vars * rows, width), BF16), vm((width, width), BF16), vm((width, 4 * HEAD), BF16),
            vm((HEAD, width), BF16), vm((width, hidden), BF16), vm((hidden, width), BF16),
            vm((rows, width), BF16), vm((rows, 128), F32),
            vm((ny, band, width), BF16), vm((ny, band, 128), F32),
            vm((2, band, width), BF16), vm((2, band, 128), F32),
            vm((band, width), F32), vm((ny, band, width), BF16),
            vm((NZ, rows, 2 * HEAD), BF16), vm((ni, rows, 2 * HEAD), BF16),
            vm((rows, width), F32),
            vm((ni, HEAD, rows), BF16), vm((ni, 8, rows), F32),
            vm((ni, HEAD, rows), BF16), vm((ni, 8, rows), F32),
            vm((ny, band, width), BF16), vm((ny, band, width), BF16),
            vm((band, width), F32), vm((band // NZH, width), F32),
            dma((6,)), dma((ny,)), dma((ny,)), dma((ny,)), dma((ny,)), dma((3,)), dma((3,)),
            dma((ny,)), dma((ny,)), dma((NZ,)), dma((NZ,)), dma((ni,)), dma((ni,)),
            dma((ni,)), dma((ni,)), dma((ni,)), dma((ni,)), dma((ny,)), dma((ny,)),
        ],
        compiler_params=pltpu.CompilerParams(collective_id=0, has_side_effects=True),
    )(
        var_tokens.reshape(n_vars * rows, width), key_query, value_weight, qkv_cols,
        out_weight, up_weight, down_weight, norm_gain.reshape(1, width),
    )


def solution(mesh):
    placed = (
        P("var", "space", None), P(), P(), P(None, None, "var"),
        P("var", None), P(None, "var"), P("var", None), P(),
    )
    return jax.shard_map(
        per_device, mesh=mesh, in_specs=placed, out_specs=P(("space", "var"), None), check_vma=False
    )
```

time: 717 us -> 93.3 us (0.13)
  waiting for transfers between devices: 529 us -> 0 us
  blocking collectives: 115 us -> 0 us
  Pallas kernels: 0 us -> 87.5 us
  starting transfers between devices: 31 us -> 0 us
  matrix products: 14.7 us -> 0 us
  between operations: 13.2 us -> 0.04 us
    reduce_scatter x1 -> x0, waiting for transfers between devices: 246 us -> none  [per_device(): lax.psum_scatter((jnp.dot(attended, out_weight, preferred_element_type=f3...]
    all_gather x2 -> x0, waiting for transfers between devices: 244 us -> none  [the longest x1 131 us: per_device(): key_block = lax.all_gather(key_local, 'space', axis=0, tiled=True)]
    all_gather x1 -> x0, blocking collectives: 115 us -> none  [per_device(): all_features = lax.all_gather(pooled, 'var', axis=1, tiled=True)]
    pallas_call x0 -> x1, Pallas kernels: none -> 87.5 us  [per_device(): pl.pallas_call(functools.partial(kernel, ny, ni, n_vars), out_shape=jax.S...]
    all_to_all x2 -> x0, waiting for transfers between devices: 38.5 us -> none  [the longest x1 28.5 us: per_device(): lax.all_to_all(values, 'var', split_axis=2, concat_axis=0, tiled=True)]
    all_to_all x2 -> x0, starting transfers between devices: 30.9 us -> none  [the longest x1 24.6 us: per_device(): lax.all_to_all(scores, 'var', split_axis=2, concat_axis=0, tiled=True)]
    dot_general x5 -> x0, matrix products: 13.4 us -> none  [the longest x1 4.37 us: per_device(): jnp.dot(attended, out_weight, preferred_element_type=f32)]
  transfers between devices with their start and end apart: 5 -> 0, of which waited for: 5 -> 0; matrix products, arithmetic and copies ran while one was open for 2% -> 0% of each run, Pallas kernels for 0% -> 0%
where the time goes in v1:
time: 93.3 us; the launch traced here: 93.1 us
  Pallas kernels  87.5 us (94%)
  local copies, waits for them, and re-layouts  4.42 us (5%)
  other arithmetic  1.07 us (1%)
    pallas_call x1, Pallas kernels, per_device(): pl.pallas_call(functools.partial(kernel, ny, ni, n_vars), out_shape=jax.S...  87.5 us
    unnamed x9, local copies, waits for them, and re-layouts  2.68 us

profile of v1, /device:TPU:1, one launch (start us, length us, event | category | flops | bytes accessed | tf_op | source)
XLA Modules:
  0.0 93.1 jit_solution(15260278869535117732)
XLA Ops:
  0.0 0.0 copy-start
  0.0 0.0 copy-start.1
  0.0 1.1 %fusion = (bf16[1024,1,64]{0,2,1:T(8,128)(2,1)S(1)}, bf16[1024,1,64]{0,2,1:T(8,128)(2,1)S(1)}, bf16[1024,1,64]{0,2,1:T(8,128)(2,1)S(1)}) fusion(bf16[1024,3,64]{0,2,1:T(8,128)(2,1)} %param.11), kind=kLoop, calls=%fused_computation.1 | loop fusion | bytes 786432 | tf_op jit(solution)/shard_map/slice | solution.py:271
  1.1 0.2 copy.13
  1.2 0.2 copy.14
  1.4 0.2 copy.15
  1.6 0.1 pad.3.clone
  1.7 1.1 %maximum_maximum_fusion.qkv_hbm = bf16[1024,256]{1,0:T(8,128)(2,1)} fusion(bf16[1024,64]{1,0:T(8,128)(2,1)S(1)} %bitcast.6, bf16[1024,64]{1,0:T(8,128)(2,1)S(1)} %bitcast.5, bf16[1024,64]{1,0:T(8,128)(2,1)S(1)} %bitcast.4, bf16[256]{0:T(256)(128)(2,1)S(1)} %pad.3.clone), kind=kLoop, calls=%fused_computation | loop fusion | flops 2097152 | bytes 918016 | tf_op jit(solution)/shard_map/concatenate | solution.py:270
  2.8 0.0 copy-done
  2.8 0.8 copy.12.kq_ref
  3.6 0.0 copy-done.1
  3.6 0.6 reshape.7.gain_ref
  4.2 87.5 %shard_map.82 = bf16[8,1024]{1,0:T(8,128)(2,1)} custom-call(bf16[512,1024]{1,0:T(8,128)(2,1)} %bitcast.7, bf16[1024,16]{1,0:T(8,128)(2,1)} %copy.12.kq_ref, bf16[1024,1024]{1,0:T(8,128)(2,1)} %vw_hbm.1, bf16[1024,256]{1,0:T(8,128)(2,1)} %maximum_maximum_fusion.qkv_hbm, bf16[64,1024]{1,0:T(8,128)(2,1)} %ow_hbm.1, bf16[1024,256]{1,0:T(8,128)(2,1)} %up_hbm.1, ...), custom_call_target="tpu_custom_call" | custom-call | tf_op jit(solution)/shard_map/pallas_call | solution.py:277
  91.7 1.3 %copy.17 = bf16[8,1024]{1,0:T(8,128)(2,1)} copy(bf16[8,1024]{1,0:T(8,128)(2,1)} %shard_map.82) | data formatting | bytes 32768
  (1 shorter events, 0.0 us)
Async XLA Ops:
  0.0 2.8 %copy-start = (bf16[1024,16]{0,1:T(8,128)(2,1)S(1)}, bf16[1024,16]{0,1:T(8,128)(2,1)}, u32[]{:S(2)}) copy-start(bf16[1024,16]{0,1:T(8,128)(2,1)} %param.9) | copy-start | bytes 98308
  0.0 3.6 %copy-start.1 = (bf16[1024]{0:T(1024)(128)(2,1)S(1)}, bf16[1024]{0:T(1024)(128)(2,1)}, u32[]{:S(2)}) copy-start(bf16[1024]{0:T(1024)(128)(2,1)} %param.15) | copy-start | bytes 6148

commit v2 on v1

v2 whole, which is shorter than its diff:
```python
import functools

import jax
import jax.numpy as jnp
from jax import lax
from jax.experimental import pallas as pl
from jax.experimental.pallas import tpu as pltpu
from jax.sharding import PartitionSpec as P

MESH = pl.DeviceIdType.MESH
F32 = jnp.float32
BF16 = jnp.bfloat16
HEAD = 64
NZH = 2
NZ = 8
NCORE = 2
CHUNKS = 2
TRANSPOSED = (((1,), (1,)), ((), ()))


def _dot(a, b, dims=(((1,), (0,)), ((), ()))):
    return lax.dot_general(a, b, dims, preferred_element_type=F32)


def _expander(heads, width):
    row = lax.broadcasted_iota(jnp.int32, (heads, width), 0)
    col = lax.broadcasted_iota(jnp.int32, (heads, width), 1)
    return jnp.where(col // HEAD == row, 1.0, 0.0).astype(BF16)


def _shares(lses):
    top = functools.reduce(jnp.maximum, lses)
    weights = [jnp.exp(lse - top) for lse in lses]
    total = functools.reduce(jnp.add, weights)
    return [w / total for w in weights], top + jnp.log(total)


def _widen(shares, spread):
    high = [s.astype(BF16) for s in shares]
    low = [(s - h.astype(F32)).astype(BF16) for s, h in zip(shares, high)]
    wide = _dot(jnp.concatenate(high + low, axis=0), spread)
    half = wide.shape[0] // 2
    return wide[:half] + wide[half:]


def _weigh(outs, wide):
    rows = outs[0].shape[0]
    terms = [wide[k * rows : (k + 1) * rows] * out.astype(F32) for k, out in enumerate(outs)]
    return functools.reduce(jnp.add, terms)


def kernel(
    ny, ni, n_vars,
    tok_hbm, kq_hbm, vw_hbm, qkv_hbm, ow_hbm, up_hbm, dw_hbm, gain_ref,
    out_ref,
    tok, kq, vw, qkvw, ow, up, dw,
    part, stat, rpart, rstat, zpart, zstat, pooled, nbuf, kvbuf, qbuf, mlp,
    near_out, near_stat, obuf, ostat, robuf, rostat, fbuf, rf, zsum, zsend, zrecv,
    load_sem, a_send, a_recv, as_send, as_recv, z_send, z_recv, n_send, n_recv,
    k_send, k_recv, q_send, q_recv, o_send, o_recv, os_send, os_recv, f_send, f_recv,
):
    rows = tok.shape[0] // n_vars
    width = tok.shape[1]
    heads = width // HEAD
    band = rows // ny
    cols = width // CHUNKS

    space = lax.axis_index("space")
    var = lax.axis_index("var")
    y, zh = var // NZH, lax.rem(var, NZH)
    z = lax.rem(space // NCORE, NZ)
    i = (space // (NCORE * NZ)) * NCORE + lax.rem(space, NCORE)

    def at_y(d):
        return {"space": space, "var": lax.rem(y + d + ny, ny) * NZH + zh}

    def at_zh():
        return {"space": space, "var": y * NZH + (1 - zh)}

    def at_z(t):
        other, bit = 0, 1
        while bit < NZ:
            mine = lax.rem(z // bit, 2)
            other = other + bit * ((1 - mine) if t & bit else mine)
            bit *= 2
        return {
            "space": (i // NCORE) * (NCORE * NZ) + other * NCORE + lax.rem(i, NCORE),
            "var": var,
        }

    def at_i(d):
        other = lax.rem(i + d + ni, ni)
        return {
            "space": (other // NCORE) * (NCORE * NZ) + z * NCORE + lax.rem(other, NCORE),
            "var": var,
        }

    started = []

    def remote(src, dst, send, recv, peer):
        return pltpu.make_async_remote_copy(
            src_ref=src, dst_ref=dst, send_sem=send, recv_sem=recv,
            device_id=peer, device_id_type=MESH,
        )

    def go(*args):
        copy = remote(*args)
        copy.start()
        started.append(copy)
        return copy

    def far_first(n):
        return sorted(range(1, n), key=lambda d: -min(d, n - d))

    moves = [(tok_hbm, tok), (kq_hbm, kq)]
    moves += [(vw_hbm.at[:, c * cols : (c + 1) * cols], vw.at[c]) for c in range(CHUNKS)]
    moves += [
        (qkv_hbm.at[:HEAD], qkvw.at[2 * HEAD : 3 * HEAD]),
        (qkv_hbm.at[HEAD:], qkvw.at[: 2 * HEAD]),
        (up_hbm, up), (dw_hbm, dw), (ow_hbm, ow),
    ]
    loads = [pltpu.make_async_copy(src, dst, load_sem.at[k]) for k, (src, dst) in enumerate(moves)]
    barrier = pltpu.get_barrier_semaphore()
    greeted = 0
    for peers in (
        [at_zh()], [at_z(t) for t in range(1, NZ)],
        [at_y(d) for d in range(1, ny)], [at_i(d) for d in range(1, ni)],
    ):
        for peer in peers:
            pl.semaphore_signal(barrier, inc=1, device_id=peer, device_id_type=MESH)
            greeted += 1
    for load in loads:
        load.start()

    spread = _expander(heads, width)
    stat[...] = jnp.zeros_like(stat)
    zstat[0] = jnp.zeros_like(zstat[0])
    loads[0].wait()
    loads[1].wait()
    scores = _dot(tok[...], kq[...], TRANSPOSED)
    per_var = [scores[v * rows : (v + 1) * rows] for v in range(n_vars)]
    top = functools.reduce(jnp.maximum, per_var)
    exps = [jnp.exp(s - top) for s in per_var]
    total = functools.reduce(jnp.add, exps)
    stat[:, :heads] = top + jnp.log(total)
    shares = jnp.concatenate([(e / total).astype(BF16) for e in exps], axis=0)

    a_copies, stat_copies = [], []
    tile = min(256, cols)
    for c in range(CHUNKS):
        loads[2 + c].wait()
        for k in range(0, cols, tile):
            values = _dot(tok[...], vw[c, :, k : k + tile]).astype(BF16).astype(F32)
            weighted = values * _dot(shares, spread[:, c * cols + k : c * cols + k + tile])
            acc = weighted[:rows]
            for v in range(1, n_vars):
                acc = acc + weighted[v * rows : (v + 1) * rows]
            part[c, :, k : k + tile] = acc.astype(BF16)
        if c == 0:
            pl.semaphore_wait(barrier, greeted)
        a_copies.append([])
        for d in far_first(ny):
            theirs = pl.ds(pl.multiple_of(lax.rem(y + d, ny) * band, band), band)
            if c == 0:
                stat_copies.append(
                    go(stat.at[theirs], rstat.at[d], as_send.at[d], as_recv.at[d], at_y(d))
                )
            a_copies[c].append(
                go(part.at[c, theirs], rpart.at[c, d], a_send.at[c, d], a_recv.at[c, d], at_y(d))
            )

    mine = pl.ds(pl.multiple_of(y * band, band), band)
    for copy in stat_copies:
        copy.wait_recv()
    shares, lse = _shares(
        [stat[mine, :][:, :heads]] + [rstat[d][:, :heads] for d in range(1, ny)]
    )
    zstat[0, :, :heads] = lse
    stat_copy = go(zstat.at[0], zstat.at[1], z_send.at[0], z_recv.at[0], at_zh())
    wide = _widen(shares, spread)
    z_copies = []
    for c in range(CHUNKS):
        for copy in a_copies[c]:
            copy.wait_recv()
        zpart[c, 0] = _weigh(
            [part[c, mine, :]] + [rpart[c, d] for d in range(1, ny)],
            wide[:, c * cols : (c + 1) * cols],
        ).astype(BF16)
        z_copies.append(
            go(zpart.at[c, 0], zpart.at[c, 1], z_send.at[1 + c], z_recv.at[1 + c], at_zh())
        )
    stat_copy.wait_recv()
    shares, _ = _shares([zstat[0][:, :heads], zstat[1][:, :heads]])
    wide = _widen(shares, spread)
    for c in range(CHUNKS):
        z_copies[c].wait_recv()
        cut = slice(c * cols, (c + 1) * cols)
        merged = _weigh([zpart[c, 0], zpart[c, 1]], wide[:, cut])
        pooled[:, cut] = merged.astype(BF16).astype(F32)
    rounded = pooled[...]
    centred = rounded - jnp.mean(rounded, axis=1, keepdims=True)
    spread_sq = jnp.mean(centred * centred, axis=1, keepdims=True)
    gain = gain_ref[...].astype(F32).reshape(1, width)
    nbuf[0] = (centred * lax.rsqrt(spread_sq + 1e-05) * gain).astype(BF16)

    copies = [
        go(nbuf.at[0], nbuf.at[d], n_send.at[d], n_recv.at[d], at_y(d)) for d in far_first(ny)
    ]
    qkvw[3 * HEAD :] = jnp.zeros_like(qkvw[3 * HEAD :])
    for load in loads[2 + CHUNKS :]:
        load.wait()
    for copy in copies:
        copy.wait_recv()
    normed = nbuf[...].reshape(rows, width)

    qkv = _dot(normed, qkvw[...], TRANSPOSED)
    kvbuf[0] = qkv[:, : 2 * HEAD].astype(BF16)
    qbuf[0] = (qkv[:, 2 * HEAD :] * HEAD**-0.5).astype(BF16)
    k_copies = {
        t: go(kvbuf.at[0], kvbuf.at[t], k_send.at[t], k_recv.at[t], at_z(t))
        for t in range(NZ - 1, 0, -1)
    }
    q_copies = [
        go(qbuf.at[0], qbuf.at[d], q_send.at[d], q_recv.at[d], at_i(d)) for d in far_first(ni)
    ]
    hidden = jax.nn.gelu(_dot(normed, up[...]), approximate=True).astype(BF16)
    mlp[...] = _dot(hidden, dw[...])

    keys = NZ // 2 * rows

    def logits_of(kv, p):
        return _dot(kv, qbuf[pl.ds(2 * p, 2)].reshape(2 * rows, 2 * HEAD), TRANSPOSED)

    for copy in q_copies:
        copy.wait_recv()
    for t in range(1, NZ // 2):
        k_copies[t].wait_recv()
    near = kvbuf[: NZ // 2].reshape(keys, 2 * HEAD)
    near_values = near.T[HEAD:]

    @pl.loop(0, ni // 2)
    def _(p):
        logits = logits_of(near, p)
        top = jnp.max(logits, axis=0, keepdims=True)
        exps = jnp.exp(logits - top)
        total = jnp.sum(exps, axis=0, keepdims=True)
        near_out[p] = _dot(near_values, exps.astype(BF16))
        near_stat[p, :8] = jnp.broadcast_to(top, (8, 2 * rows))
        near_stat[p, 8:] = jnp.broadcast_to(total, (8, 2 * rows))

    for t in range(NZ // 2, NZ):
        k_copies[t].wait_recv()
    far = kvbuf[NZ // 2 :].reshape(keys, 2 * HEAD)
    far_values = far.T[HEAD:]

    def finish(p):
        logits = logits_of(far, p)
        near_top = near_stat[p, :1]
        top = jnp.maximum(near_top, jnp.max(logits, axis=0, keepdims=True))
        exps = jnp.exp(logits - top)
        scale = jnp.exp(near_top - top)
        total = jnp.sum(exps, axis=0, keepdims=True) + scale * near_stat[p, 8:9]
        out = (_dot(far_values, exps.astype(BF16)) + scale * near_out[p]) / total
        lse = jnp.broadcast_to(top + jnp.log(total), (8, 2 * rows))
        for k in range(2):
            obuf[2 * p + k] = out[:, k * rows : (k + 1) * rows].astype(BF16)
            ostat[2 * p + k] = lse[:, k * rows : (k + 1) * rows]

    def give(d):
        owner = at_i(-d)
        return (
            remote(obuf.at[d], robuf.at[d], o_send.at[d], o_recv.at[d], owner),
            remote(ostat.at[d], rostat.at[d], os_send.at[d], os_recv.at[d], owner),
        )

    @pl.loop(1, ni // 2)
    def _(p):
        finish(p)
        for k in range(2):
            for copy in give(2 * p + k):
                copy.start()

    finish(0)
    for copy in give(1):
        copy.start()
    for d in range(1, ni):
        for copy in give(d):
            started.append(copy)
            copy.wait_recv()
    shares, _ = _shares([ostat[0][:1]] + [rostat[d][:1] for d in range(1, ni)])
    attended = obuf[0].astype(F32) * shares[0]
    for d in range(1, ni):
        attended = attended + robuf[d].astype(F32) * shares[d]

    attended = attended.T.astype(BF16)
    f_copies = []
    for c in range(CHUNKS):
        cut = slice(c * cols, (c + 1) * cols)
        term = _dot(attended, ow[:, cut]) + mlp[:, cut]
        zsum[:, cut] = term[:band]
        fbuf[c] = term.reshape(ny, band, cols).astype(BF16)
        f_copies.append([
            go(fbuf.at[c, d], rf.at[c, d], f_send.at[c, d], f_recv.at[c, d], at_y(-d))
            for d in far_first(ny)
        ])
    half = band // NZH
    own = pl.ds(pl.multiple_of(zh * half, half), half)
    other = pl.ds(pl.multiple_of((1 - zh) * half, half), half)
    z_copies = []
    for c in range(CHUNKS):
        cut = slice(c * cols, (c + 1) * cols)
        for copy in f_copies[c]:
            copy.wait_recv()
        summed = zsum[:, cut]
        for d in range(1, ny):
            summed = summed + rf[c, d].astype(F32)
        zsum[:, cut] = summed
        zsend[c] = zsum[other, cut].astype(BF16)
        sem = 1 + CHUNKS + c
        z_copies.append(go(zsend.at[c], zrecv.at[c], z_send.at[sem], z_recv.at[sem], at_zh()))
    for c in range(CHUNKS):
        cut = slice(c * cols, (c + 1) * cols)
        z_copies[c].wait_recv()
        out_ref[:, cut] = (
            pooled[own, cut] + (zsum[own, cut] + zrecv[c].astype(F32))
        ).astype(BF16)
    for copy in started:
        copy.wait_send()


def per_device(var_tokens, key_query, value_weight, qkv_weight, out_weight, up_weight, down_weight, norm_gain):
    n_vars, rows, width = var_tokens.shape
    ny = lax.axis_size("var") // NZH
    ni = lax.axis_size("space") // NZ
    band = rows // ny
    hidden = up_weight.shape[1]
    cols = width // CHUNKS
    half = band // NZH
    any_spec = pl.BlockSpec(memory_space=pl.ANY)
    vmem_spec = pl.BlockSpec(memory_space=pltpu.VMEM)
    dma = pltpu.SemaphoreType.DMA
    vm = pltpu.VMEM
    return pl.pallas_call(
        functools.partial(kernel, ny, ni, n_vars),
        out_shape=jax.ShapeDtypeStruct((half, width), BF16),
        in_specs=[any_spec] * 7 + [vmem_spec],
        out_specs=vmem_spec,
        scratch_shapes=[
            vm((n_vars * rows, width), BF16), vm(key_query.shape[::-1], BF16), vm((CHUNKS, width, cols), BF16),
            vm((4 * HEAD, width), BF16), vm((HEAD, width), BF16), vm((width, hidden), BF16), vm((hidden, width), BF16),
            vm((CHUNKS, rows, cols), BF16), vm((rows, 128), F32),
            vm((CHUNKS, ny, band, cols), BF16), vm((ny, band, 128), F32),
            vm((CHUNKS, 2, band, cols), BF16), vm((2, band, 128), F32),
            vm((band, width), F32), vm((ny, band, width), BF16),
            vm((NZ, rows, 2 * HEAD), BF16), vm((ni, rows, 2 * HEAD), BF16),
            vm((rows, width), F32),
            vm((ni // 2, HEAD, 2 * rows), F32), vm((ni // 2, 16, 2 * rows), F32),
            vm((ni, HEAD, rows), BF16), vm((ni, 8, rows), F32),
            vm((ni, HEAD, rows), BF16), vm((ni, 8, rows), F32),
            vm((CHUNKS, ny, band, cols), BF16), vm((CHUNKS, ny, band, cols), BF16),
            vm((band, width), F32), vm((CHUNKS, half, cols), BF16), vm((CHUNKS, half, cols), BF16),
            dma((7 + CHUNKS,)), dma((CHUNKS, ny)), dma((CHUNKS, ny)), dma((ny,)), dma((ny,)),
            dma((1 + 2 * CHUNKS,)), dma((1 + 2 * CHUNKS,)),
            dma((ny,)), dma((ny,)), dma((NZ,)), dma((NZ,)), dma((ni,)), dma((ni,)),
            dma((ni,)), dma((ni,)), dma((ni,)), dma((ni,)), dma((CHUNKS, ny)), dma((CHUNKS, ny)),
        ],
        compiler_params=pltpu.CompilerParams(collective_id=0, has_side_effects=True),
    )(
        var_tokens.reshape(n_vars * rows, width), key_query.T, value_weight,
        qkv_weight.transpose(1, 2, 0).reshape(3 * HEAD, width),
        out_weight, up_weight, down_weight, norm_gain,
    )


def solution(mesh):
    placed = (
        P("var", "space", None), P(), P(), P(None, None, "var"),
        P("var", None), P(None, "var"), P("var", None), P(),
    )
    return jax.shard_map(
        per_device, mesh=mesh, in_specs=placed, out_specs=P(("space", "var"), None), check_vma=False
    )
```

time: 93.3 us -> 84.2 us (0.902)
  Pallas kernels: 87.5 us -> 81.8 us
  local copies, waits for them, and re-layouts: 4.42 us -> 1.32 us
  other arithmetic: 1.07 us -> 0 us
    pallas_call x1, Pallas kernels: 87.5 us -> 81.8 us  [per_device(): pl.pallas_call(functools.partial(kernel, ny, ni, n_vars), out_shape=jax.S...]
    unnamed x9 -> x1, local copies, waits for them, and re-layouts: 2.68 us -> 1.32 us
    concatenate x1 -> x0, other arithmetic: 1.07 us -> none  [per_device(): jnp.concatenate([qkv_weight[:, 1], qkv_weight[:, 2], qkv_weight[:, 0], bl...]
    slice x1 -> x0, local copies, waits for them, and re-layouts: 1.06 us -> none  [per_device(): qkv_weight[:, 1]]
where the time goes in v2:
time: 84.2 us; the launch traced here: 83.1 us
  Pallas kernels  81.8 us (97%)
  local copies, waits for them, and re-layouts  1.32 us (2%)
    pallas_call x1, Pallas kernels, per_device(): pl.pallas_call(functools.partial(kernel, ny, ni, n_vars), out_shape=jax.S...  81.8 us

profile of v2, /device:TPU:1, one launch (start us, length us, event | category | flops | bytes accessed | tf_op | source)
XLA Modules:
  0.0 83.1 jit_solution(12722287006589429043)
XLA Ops:
  0.0 81.8 %shard_map.82 = bf16[8,1024]{1,0:T(8,128)(2,1)} custom-call(bf16[512,1024]{1,0:T(8,128)(2,1)} %bitcast.5, bf16[16,1024]{1,0:T(8,128)(2,1)} %bitcast.7, bf16[1024,1024]{1,0:T(8,128)(2,1)} %vw_hbm.1, bf16[192,1024]{1,0:T(8,128)(2,1)} %bitcast.6, bf16[64,1024]{1,0:T(8,128)(2,1)} %ow_hbm.1, bf16[1024,256]{1,0:T(8,128)(2,1)} %up_hbm.1, bf16[256,1024]{1,0:T(8,128)(2,1)} %dw_hbm.1, ...), custom_call_target="tpu_custom_call" | custom-call | tf_op jit(solution)/shard_map/pallas_call | solution.py:343
  81.8 1.3 %copy.10 = bf16[8,1024]{1,0:T(8,128)(2,1)} copy(bf16[8,1024]{1,0:T(8,128)(2,1)} %shard_map.82) | data formatting | bytes 32768

commit v3 on v2

--- a/solution.py
+++ b/solution.py
@@ -14,7 +14,8 @@
 NZH = 2
 NZ = 8
 NCORE = 2
-CHUNKS = 2
+CHUNKS = 4
+GROUP = 4
 TRANSPOSED = (((1,), (1,)), ((), ()))
 
 
@@ -41,6 +42,16 @@
     wide = _dot(jnp.concatenate(high + low, axis=0), spread)
     half = wide.shape[0] // 2
     return wide[:half] + wide[half:]
+
+
+def _pack(lse):
+    *lead, rows, heads = lse.shape
+    pair = lse.reshape(*lead, 2, rows // 2, heads)
+    return jnp.concatenate([pair[..., 0, :, :], pair[..., 1, :, :]], axis=-1)
+
+
+def _unpack(packed, heads):
+    return jnp.concatenate([packed[:, :heads], packed[:, heads : 2 * heads]], axis=0)
 
 
 def _weigh(outs, wide):
@@ -142,7 +153,7 @@
     top = functools.reduce(jnp.maximum, per_var)
     exps = [jnp.exp(s - top) for s in per_var]
     total = functools.reduce(jnp.add, exps)
-    stat[:, :heads] = top + jnp.log(total)
+    stat[:, :, : 2 * heads] = _pack((top + jnp.log(total)).reshape(ny, band, heads))
     shares = jnp.concatenate([(e / total).astype(BF16) for e in exps], axis=0)
 
     a_copies, stat_copies = [], []
@@ -160,10 +171,11 @@
             pl.semaphore_wait(barrier, greeted)
         a_copies.append([])
         for d in far_first(ny):
-            theirs = pl.ds(pl.multiple_of(lax.rem(y + d, ny) * band, band), band)
+            peer = lax.rem(y + d, ny)
+            theirs = pl.ds(pl.multiple_of(peer * band, band), band)
             if c == 0:
                 stat_copies.append(
-                    go(stat.at[theirs], rstat.at[d], as_send.at[d], as_recv.at[d], at_y(d))
+                    go(stat.at[peer], rstat.at[d], as_send.at[d], as_recv.at[d], at_y(d))
                 )
             a_copies[c].append(
                 go(part.at[c, theirs], rpart.at[c, d], a_send.at[c, d], a_recv.at[c, d], at_y(d))
@@ -173,9 +185,9 @@
     for copy in stat_copies:
         copy.wait_recv()
     shares, lse = _shares(
-        [stat[mine, :][:, :heads]] + [rstat[d][:, :heads] for d in range(1, ny)]
+        [_unpack(stat[y], heads)] + [_unpack(rstat[d], heads) for d in range(1, ny)]
     )
-    zstat[0, :, :heads] = lse
+    zstat[0, :, : 2 * heads] = _pack(lse)
     stat_copy = go(zstat.at[0], zstat.at[1], z_send.at[0], z_recv.at[0], at_zh())
     wide = _widen(shares, spread)
     z_copies = []
@@ -190,7 +202,7 @@
             go(zpart.at[c, 0], zpart.at[c, 1], z_send.at[1 + c], z_recv.at[1 + c], at_zh())
         )
     stat_copy.wait_recv()
-    shares, _ = _shares([zstat[0][:, :heads], zstat[1][:, :heads]])
+    shares, _ = _shares([_unpack(zstat[k], heads) for k in range(2)])
     wide = _widen(shares, spread)
     for c in range(CHUNKS):
         z_copies[c].wait_recv()
@@ -227,9 +239,12 @@
     mlp[...] = _dot(hidden, dw[...])
 
     keys = NZ // 2 * rows
+    group = min(GROUP, ni)
+    wide_rows = group * rows
+    order = range(ni // group - 1, -1, -1)
 
     def logits_of(kv, p):
-        return _dot(kv, qbuf[pl.ds(2 * p, 2)].reshape(2 * rows, 2 * HEAD), TRANSPOSED)
+        return _dot(kv, qbuf[p * group : (p + 1) * group].reshape(wide_rows, 2 * HEAD), TRANSPOSED)
 
     for copy in q_copies:
         copy.wait_recv()
@@ -238,15 +253,14 @@
     near = kvbuf[: NZ // 2].reshape(keys, 2 * HEAD)
     near_values = near.T[HEAD:]
 
-    @pl.loop(0, ni // 2)
-    def _(p):
+    for p in order:
         logits = logits_of(near, p)
         top = jnp.max(logits, axis=0, keepdims=True)
         exps = jnp.exp(logits - top)
         total = jnp.sum(exps, axis=0, keepdims=True)
         near_out[p] = _dot(near_values, exps.astype(BF16))
-        near_stat[p, :8] = jnp.broadcast_to(top, (8, 2 * rows))
-        near_stat[p, 8:] = jnp.broadcast_to(total, (8, 2 * rows))
+        near_stat[p, :8] = jnp.broadcast_to(top, (8, wide_rows))
+        near_stat[p, 8:] = jnp.broadcast_to(total, (8, wide_rows))
 
     for t in range(NZ // 2, NZ):
         k_copies[t].wait_recv()
@@ -261,69 +275,52 @@
         scale = jnp.exp(near_top - top)
         total = jnp.sum(exps, axis=0, keepdims=True) + scale * near_stat[p, 8:9]
         out = (_dot(far_values, exps.astype(BF16)) + scale * near_out[p]) / total
-        lse = jnp.broadcast_to(top + jnp.log(total), (8, 2 * rows))
-        for k in range(2):
-            obuf[2 * p + k] = out[:, k * rows : (k + 1) * rows].astype(BF16)
-            ostat[2 * p + k] = lse[:, k * rows : (k + 1) * rows]
-
-    def give(d):
-        owner = at_i(-d)
-        return (
-            remote(obuf.at[d], robuf.at[d], o_send.at[d], o_recv.at[d], owner),
-            remote(ostat.at[d], rostat.at[d], os_send.at[d], os_recv.at[d], owner),
-        )
-
-    @pl.loop(1, ni // 2)
-    def _(p):
+        lse = jnp.broadcast_to(top + jnp.log(total), (8, wide_rows))
+        for k in range(group):
+            obuf[group * p + k] = out[:, k * rows : (k + 1) * rows].astype(BF16)
+            ostat[group * p + k] = lse[:, k * rows : (k + 1) * rows]
+
+    returns = []
+    for p in order:
         finish(p)
-        for k in range(2):
-            for copy in give(2 * p + k):
-                copy.start()
-
-    finish(0)
-    for copy in give(1):
-        copy.start()
-    for d in range(1, ni):
-        for copy in give(d):
-            started.append(copy)
-            copy.wait_recv()
+        for d in range(max(1, p * group), (p + 1) * group):
+            owner = at_i(-d)
+            returns.append(go(obuf.at[d], robuf.at[d], o_send.at[d], o_recv.at[d], owner))
+            returns.append(go(ostat.at[d], rostat.at[d], os_send.at[d], os_recv.at[d], owner))
+    for copy in returns:
+        copy.wait_recv()
     shares, _ = _shares([ostat[0][:1]] + [rostat[d][:1] for d in range(1, ni)])
     attended = obuf[0].astype(F32) * shares[0]
     for d in range(1, ni):
         attended = attended + robuf[d].astype(F32) * shares[d]
 
-    attended = attended.T.astype(BF16)
+    term = _dot(attended.T.astype(BF16), ow[...]) + mlp[...]
+    half = band // NZH
+    bands = term.reshape(ny, NZH, half, width)
+    for h in range(NZH):
+        fbuf[h] = bands[:, h].astype(BF16)
+        zsum[h] = bands[0, h]
     f_copies = []
-    for c in range(CHUNKS):
-        cut = slice(c * cols, (c + 1) * cols)
-        term = _dot(attended, ow[:, cut]) + mlp[:, cut]
-        zsum[:, cut] = term[:band]
-        fbuf[c] = term.reshape(ny, band, cols).astype(BF16)
+    for stage, h in enumerate((1 - zh, zh)):
         f_copies.append([
-            go(fbuf.at[c, d], rf.at[c, d], f_send.at[c, d], f_recv.at[c, d], at_y(-d))
+            go(fbuf.at[h, d], rf.at[stage, d], f_send.at[stage, d], f_recv.at[stage, d], at_y(-d))
             for d in far_first(ny)
         ])
-    half = band // NZH
+
+    def summed(stage, h):
+        for copy in f_copies[stage]:
+            copy.wait_recv()
+        total = zsum[h]
+        for d in range(1, ny):
+            total = total + rf[stage, d].astype(F32)
+        return total
+
+    zsend[...] = summed(0, 1 - zh).astype(BF16)
+    last = go(zsend, zrecv, z_send.at[1 + CHUNKS], z_recv.at[1 + CHUNKS], at_zh())
     own = pl.ds(pl.multiple_of(zh * half, half), half)
-    other = pl.ds(pl.multiple_of((1 - zh) * half, half), half)
-    z_copies = []
-    for c in range(CHUNKS):
-        cut = slice(c * cols, (c + 1) * cols)
-        for copy in f_copies[c]:
-            copy.wait_recv()
-        summed = zsum[:, cut]
-        for d in range(1, ny):
-            summed = summed + rf[c, d].astype(F32)
-        zsum[:, cut] = summed
-        zsend[c] = zsum[other, cut].astype(BF16)
-        sem = 1 + CHUNKS + c
-        z_copies.append(go(zsend.at[c], zrecv.at[c], z_send.at[sem], z_recv.at[sem], at_zh()))
-    for c in range(CHUNKS):
-        cut = slice(c * cols, (c + 1) * cols)
-        z_copies[c].wait_recv()
-        out_ref[:, cut] = (
-            pooled[own, cut] + (zsum[own, cut] + zrecv[c].astype(F32))
-        ).astype(BF16)
+    mine = summed(1, zh) + pooled[own, :]
+    last.wait_recv()
+    out_ref[...] = (mine + zrecv[...].astype(F32)).astype(BF16)
     for copy in started:
         copy.wait_send()
 
@@ -336,6 +333,7 @@
     hidden = up_weight.shape[1]
     cols = width // CHUNKS
     half = band // NZH
+    group = min(GROUP, ni)
     any_spec = pl.BlockSpec(memory_space=pl.ANY)
     vmem_spec = pl.BlockSpec(memory_space=pltpu.VMEM)
     dma = pltpu.SemaphoreType.DMA
@@ -348,21 +346,21 @@
         scratch_shapes=[
             vm((n_vars * rows, width), BF16), vm(key_query.shape[::-1], BF16), vm((CHUNKS, width, cols), BF16),
             vm((4 * HEAD, width), BF16), vm((HEAD, width), BF16), vm((width, hidden), BF16), vm((hidden, width), BF16),
-            vm((CHUNKS, rows, cols), BF16), vm((rows, 128), F32),
-            vm((CHUNKS, ny, band, cols), BF16), vm((ny, band, 128), F32),
-            vm((CHUNKS, 2, band, cols), BF16), vm((2, band, 128), F32),
+            vm((CHUNKS, rows, cols), BF16), vm((ny, band // 2, 128), F32),
+            vm((CHUNKS, ny, band, cols), BF16), vm((ny, band // 2, 128), F32),
+            vm((CHUNKS, 2, band, cols), BF16), vm((2, band // 2, 128), F32),
             vm((band, width), F32), vm((ny, band, width), BF16),
             vm((NZ, rows, 2 * HEAD), BF16), vm((ni, rows, 2 * HEAD), BF16),
             vm((rows, width), F32),
-            vm((ni // 2, HEAD, 2 * rows), F32), vm((ni // 2, 16, 2 * rows), F32),
+            vm((ni // group, HEAD, group * rows), F32), vm((ni // group, 16, group * rows), F32),
             vm((ni, HEAD, rows), BF16), vm((ni, 8, rows), F32),
             vm((ni, HEAD, rows), BF16), vm((ni, 8, rows), F32),
-            vm((CHUNKS, ny, band, cols), BF16), vm((CHUNKS, ny, band, cols), BF16),
-            vm((band, width), F32), vm((CHUNKS, half, cols), BF16), vm((CHUNKS, half, cols), BF16),
+            vm((NZH, ny, half, width), BF16), vm((NZH, ny, half, width), BF16),
+            vm((NZH, half, width), F32), vm((half, width), BF16), vm((half, width), BF16),
             dma((7 + CHUNKS,)), dma((CHUNKS, ny)), dma((CHUNKS, ny)), dma((ny,)), dma((ny,)),
-            dma((1 + 2 * CHUNKS,)), dma((1 + 2 * CHUNKS,)),
+            dma((2 + CHUNKS,)), dma((2 + CHUNKS,)),
             dma((ny,)), dma((ny,)), dma((NZ,)), dma((NZ,)), dma((ni,)), dma((ni,)),
-            dma((ni,)), dma((ni,)), dma((ni,)), dma((ni,)), dma((CHUNKS, ny)), dma((CHUNKS, ny)),
+            dma((ni,)), dma((ni,)), dma((ni,)), dma((ni,)), dma((NZH, ny)), dma((NZH, ny)),
         ],
         compiler_params=pltpu.CompilerParams(collective_id=0, has_side_effects=True),
     )(

time: 84.2 us -> 81.1 us (0.963)
  Pallas kernels: 81.8 us -> 79.3 us
    pallas_call x1, Pallas kernels: 81.8 us -> 79.3 us  [per_device(): pl.pallas_call(functools.partial(kernel, ny, ni, n_vars), out_shape=jax.S...]
where the time goes in v3:
time: 81.1 us; the launch traced here: 80.6 us
  Pallas kernels  79.3 us (98%)
  local copies, waits for them, and re-layouts  1.32 us (2%)
    pallas_call x1, Pallas kernels, per_device(): pl.pallas_call(functools.partial(kernel, ny, ni, n_vars), out_shape=jax.S...  79.3 us

profile of v3, /device:TPU:1, one launch (start us, length us, event | category | flops | bytes accessed | tf_op | source)
XLA Modules:
  0.0 80.6 jit_solution(4729058018786801842)
XLA Ops:
  0.0 79.3 %shard_map.82 = bf16[8,1024]{1,0:T(8,128)(2,1)} custom-call(bf16[512,1024]{1,0:T(8,128)(2,1)} %bitcast.5, bf16[16,1024]{1,0:T(8,128)(2,1)} %bitcast.7, bf16[1024,1024]{1,0:T(8,128)(2,1)} %vw_hbm.1, bf16[192,1024]{1,0:T(8,128)(2,1)} %bitcast.6, bf16[64,1024]{1,0:T(8,128)(2,1)} %ow_hbm.1, bf16[1024,256]{1,0:T(8,128)(2,1)} %up_hbm.1, bf16[256,1024]{1,0:T(8,128)(2,1)} %dw_hbm.1, ...), custom_call_target="tpu_custom_call" | custom-call | tf_op jit(solution)/shard_map/pallas_call | solution.py:341
  79.3 1.3 %copy.10 = bf16[8,1024]{1,0:T(8,128)(2,1)} copy(bf16[8,1024]{1,0:T(8,128)(2,1)} %shard_map.82) | data formatting | bytes 32768

commit v4 on v3

--- a/solution.py
+++ b/solution.py
@@ -215,26 +215,35 @@
     gain = gain_ref[...].astype(F32).reshape(1, width)
     nbuf[0] = (centred * lax.rsqrt(spread_sq + 1e-05) * gain).astype(BF16)
 
-    copies = [
-        go(nbuf.at[0], nbuf.at[d], n_send.at[d], n_recv.at[d], at_y(d)) for d in far_first(ny)
-    ]
+    n_copies = {
+        d: go(nbuf.at[0], nbuf.at[d], n_send.at[d], n_recv.at[d], at_y(d))
+        for d in [*range(ny // 2 - 1, 0, -1), *range(ny // 2, ny)]
+    }
     qkvw[3 * HEAD :] = jnp.zeros_like(qkvw[3 * HEAD :])
-    for load in loads[2 + CHUNKS :]:
+    for load in loads[2 + CHUNKS : 4 + CHUNKS]:
         load.wait()
-    for copy in copies:
-        copy.wait_recv()
-    normed = nbuf[...].reshape(rows, width)
-
-    qkv = _dot(normed, qkvw[...], TRANSPOSED)
-    kvbuf[0] = qkv[:, : 2 * HEAD].astype(BF16)
-    qbuf[0] = (qkv[:, 2 * HEAD :] * HEAD**-0.5).astype(BF16)
-    k_copies = {
-        t: go(kvbuf.at[0], kvbuf.at[t], k_send.at[t], k_recv.at[t], at_z(t))
-        for t in range(NZ - 1, 0, -1)
-    }
+
+    k_copies = {t: [] for t in range(1, NZ)}
+    for h in range(2):
+        bands = range(h * ny // 2, (h + 1) * ny // 2)
+        for d in bands:
+            if d:
+                n_copies[d].wait_recv()
+        some = nbuf[bands.start : bands.stop].reshape(rows // 2, width)
+        qkv = _dot(some, qkvw[...], TRANSPOSED)
+        cut = slice(h * rows // 2, (h + 1) * rows // 2)
+        kvbuf[0, cut] = qkv[:, : 2 * HEAD].astype(BF16)
+        qbuf[0, cut] = (qkv[:, 2 * HEAD :] * HEAD**-0.5).astype(BF16)
+        for t in range(NZ - 1, 0, -1):
+            k_copies[t].append(
+                go(kvbuf.at[0, cut], kvbuf.at[t, cut], k_send.at[h, t], k_recv.at[h, t], at_z(t))
+            )
     q_copies = [
         go(qbuf.at[0], qbuf.at[d], q_send.at[d], q_recv.at[d], at_i(d)) for d in far_first(ni)
     ]
+    for load in loads[4 + CHUNKS :]:
+        load.wait()
+    normed = nbuf[...].reshape(rows, width)
     hidden = jax.nn.gelu(_dot(normed, up[...]), approximate=True).astype(BF16)
     mlp[...] = _dot(hidden, dw[...])
 
@@ -249,7 +258,8 @@
     for copy in q_copies:
         copy.wait_recv()
     for t in range(1, NZ // 2):
-        k_copies[t].wait_recv()
+        for copy in k_copies[t]:
+            copy.wait_recv()
     near = kvbuf[: NZ // 2].reshape(keys, 2 * HEAD)
     near_values = near.T[HEAD:]
 
@@ -263,7 +273,8 @@
         near_stat[p, 8:] = jnp.broadcast_to(total, (8, wide_rows))
 
     for t in range(NZ // 2, NZ):
-        k_copies[t].wait_recv()
+        for copy in k_copies[t]:
+            copy.wait_recv()
     far = kvbuf[NZ // 2 :].reshape(keys, 2 * HEAD)
     far_values = far.T[HEAD:]
 
@@ -359,7 +370,7 @@
             vm((NZH, half, width), F32), vm((half, width), BF16), vm((half, width), BF16),
             dma((7 + CHUNKS,)), dma((CHUNKS, ny)), dma((CHUNKS, ny)), dma((ny,)), dma((ny,)),
             dma((2 + CHUNKS,)), dma((2 + CHUNKS,)),
-            dma((ny,)), dma((ny,)), dma((NZ,)), dma((NZ,)), dma((ni,)), dma((ni,)),
+            dma((ny,)), dma((ny,)), dma((2, NZ)), dma((2, NZ)), dma((ni,)), dma((ni,)),
             dma((ni,)), dma((ni,)), dma((ni,)), dma((ni,)), dma((NZH, ny)), dma((NZH, ny)),
         ],
         compiler_params=pltpu.CompilerParams(collective_id=0, has_side_effects=True),

time: 81.1 us -> 81.3 us (level)
  no operation moved by 1% of the time
where the time goes in v4:
time: 81.3 us; the launch traced here: 81 us
  Pallas kernels  79.7 us (98%)
  local copies, waits for them, and re-layouts  1.32 us (2%)
    pallas_call x1, Pallas kernels, per_device(): pl.pallas_call(functools.partial(kernel, ny, ni, n_vars), out_shape=jax.S...  79.7 us

profile of v4, /device:TPU:1, one launch (start us, length us, event | category | flops | bytes accessed | tf_op | source)
XLA Modules:
  0.0 81.0 jit_solution(10502773359143636344)
XLA Ops:
  0.0 79.7 %shard_map.82 = bf16[8,1024]{1,0:T(8,128)(2,1)} custom-call(bf16[512,1024]{1,0:T(8,128)(2,1)} %bitcast.5, bf16[16,1024]{1,0:T(8,128)(2,1)} %bitcast.7, bf16[1024,1024]{1,0:T(8,128)(2,1)} %vw_hbm.1, bf16[192,1024]{1,0:T(8,128)(2,1)} %bitcast.6, bf16[64,1024]{1,0:T(8,128)(2,1)} %ow_hbm.1, bf16[1024,256]{1,0:T(8,128)(2,1)} %up_hbm.1, bf16[256,1024]{1,0:T(8,128)(2,1)} %dw_hbm.1, ...), custom_call_target="tpu_custom_call" | custom-call | tf_op jit(solution)/shard_map/pallas_call | solution.py:352
  79.7 1.3 %copy.10 = bf16[8,1024]{1,0:T(8,128)(2,1)} copy(bf16[8,1024]{1,0:T(8,128)(2,1)} %shard_map.82) | data formatting | bytes 32768

commit v5 on v3

--- a/solution.py
+++ b/solution.py
@@ -66,7 +66,7 @@
     out_ref,
     tok, kq, vw, qkvw, ow, up, dw,
     part, stat, rpart, rstat, zpart, zstat, pooled, nbuf, kvbuf, qbuf, mlp,
-    near_out, near_stat, obuf, ostat, robuf, rostat, fbuf, rf, zsum, zsend, zrecv,
+    run_out, run_stat, obuf, ostat, robuf, rostat, fbuf, rf, zsum, zsend, zrecv,
     load_sem, a_send, a_recv, as_send, as_recv, z_send, z_recv, n_send, n_recv,
     k_send, k_recv, q_send, q_recv, o_send, o_recv, os_send, os_recv, f_send, f_recv,
 ):
@@ -132,16 +132,15 @@
     ]
     loads = [pltpu.make_async_copy(src, dst, load_sem.at[k]) for k, (src, dst) in enumerate(moves)]
     barrier = pltpu.get_barrier_semaphore()
-    greeted = 0
-    for peers in (
-        [at_zh()], [at_z(t) for t in range(1, NZ)],
-        [at_y(d) for d in range(1, ny)], [at_i(d) for d in range(1, ni)],
-    ):
-        for peer in peers:
-            pl.semaphore_signal(barrier, inc=1, device_id=peer, device_id_type=MESH)
-            greeted += 1
+    far_peers = [at_zh()] + [at_z(t) for t in range(1, NZ)]
+    near_peers = [at_y(d) for d in range(1, ny)] + [at_i(d) for d in range(1, ni)]
+    greeted = len(far_peers) + len(near_peers)
+    for peer in far_peers:
+        pl.semaphore_signal(barrier, inc=1, device_id=peer, device_id_type=MESH)
     for load in loads:
         load.start()
+    for peer in near_peers:
+        pl.semaphore_signal(barrier, inc=1, device_id=peer, device_id_type=MESH)
 
     spread = _expander(heads, width)
     stat[...] = jnp.zeros_like(stat)
@@ -238,51 +237,49 @@
     hidden = jax.nn.gelu(_dot(normed, up[...]), approximate=True).astype(BF16)
     mlp[...] = _dot(hidden, dw[...])
 
-    keys = NZ // 2 * rows
     group = min(GROUP, ni)
     wide_rows = group * rows
     order = range(ni // group - 1, -1, -1)
 
-    def logits_of(kv, p):
-        return _dot(kv, qbuf[p * group : (p + 1) * group].reshape(wide_rows, 2 * HEAD), TRANSPOSED)
-
-    for copy in q_copies:
-        copy.wait_recv()
-    for t in range(1, NZ // 2):
-        k_copies[t].wait_recv()
-    near = kvbuf[: NZ // 2].reshape(keys, 2 * HEAD)
-    near_values = near.T[HEAD:]
-
-    for p in order:
-        logits = logits_of(near, p)
+    def absorb(first, stop, p):
+        kv = kvbuf[first:stop].reshape((stop - first) * rows, 2 * HEAD)
+        queries = qbuf[p * group : (p + 1) * group].reshape(wide_rows, 2 * HEAD)
+        logits = _dot(kv, queries, TRANSPOSED)
         top = jnp.max(logits, axis=0, keepdims=True)
+        if first:
+            top = jnp.maximum(top, run_stat[p, :1])
         exps = jnp.exp(logits - top)
         total = jnp.sum(exps, axis=0, keepdims=True)
-        near_out[p] = _dot(near_values, exps.astype(BF16))
-        near_stat[p, :8] = jnp.broadcast_to(top, (8, wide_rows))
-        near_stat[p, 8:] = jnp.broadcast_to(total, (8, wide_rows))
-
-    for t in range(NZ // 2, NZ):
-        k_copies[t].wait_recv()
-    far = kvbuf[NZ // 2 :].reshape(keys, 2 * HEAD)
-    far_values = far.T[HEAD:]
-
-    def finish(p):
-        logits = logits_of(far, p)
-        near_top = near_stat[p, :1]
-        top = jnp.maximum(near_top, jnp.max(logits, axis=0, keepdims=True))
-        exps = jnp.exp(logits - top)
-        scale = jnp.exp(near_top - top)
-        total = jnp.sum(exps, axis=0, keepdims=True) + scale * near_stat[p, 8:9]
-        out = (_dot(far_values, exps.astype(BF16)) + scale * near_out[p]) / total
+        out = _dot(kv.T[HEAD:], exps.astype(BF16))
+        if first:
+            scale = jnp.exp(run_stat[p, :1] - top)
+            total = total + scale * run_stat[p, 8:9]
+            out = out + scale * run_out[p]
+        if stop < NZ:
+            run_out[p] = out
+            run_stat[p, :8] = jnp.broadcast_to(top, (8, wide_rows))
+            run_stat[p, 8:] = jnp.broadcast_to(total, (8, wide_rows))
+            return
+        out = out / total
         lse = jnp.broadcast_to(top + jnp.log(total), (8, wide_rows))
         for k in range(group):
             obuf[group * p + k] = out[:, k * rows : (k + 1) * rows].astype(BF16)
             ostat[group * p + k] = lse[:, k * rows : (k + 1) * rows]
 
+    for copy in q_copies:
+        copy.wait_recv()
+    cuts = [0, NZ // 2, NZ * 3 // 4, NZ] if NZ % 4 == 0 else [0, NZ // 2, NZ]
+    for first, stop in zip(cuts[:-2], cuts[1:-1]):
+        for t in range(max(1, first), stop):
+            k_copies[t].wait_recv()
+        for p in order:
+            absorb(first, stop, p)
+    for t in range(cuts[-2], NZ):
+        k_copies[t].wait_recv()
+
     returns = []
     for p in order:
-        finish(p)
+        absorb(cuts[-2], NZ, p)
         for d in range(max(1, p * group), (p + 1) * group):
             owner = at_i(-d)
             returns.append(go(obuf.at[d], robuf.at[d], o_send.at[d], o_recv.at[d], owner))

time: 81.1 us -> 82.4 us (1.016)
  Pallas kernels: 79.3 us -> 80.8 us
    pallas_call x1, Pallas kernels: 79.3 us -> 80.8 us  [per_device(): pl.pallas_call(functools.partial(kernel, ny, ni, n_vars), out_shape=jax.S...]
where the time goes in v5:
time: 82.4 us; the launch traced here: 82.1 us
  Pallas kernels  80.8 us (98%)
  local copies, waits for them, and re-layouts  1.32 us (2%)
    pallas_call x1, Pallas kernels, per_device(): pl.pallas_call(functools.partial(kernel, ny, ni, n_vars), out_shape=jax.S...  80.8 us

profile of v5, /device:TPU:1, one launch (start us, length us, event | category | flops | bytes accessed | tf_op | source)
XLA Modules:
  0.0 82.1 jit_solution(2888445525633062417)
XLA Ops:
  0.0 80.8 %shard_map.82 = bf16[8,1024]{1,0:T(8,128)(2,1)} custom-call(bf16[512,1024]{1,0:T(8,128)(2,1)} %bitcast.5, bf16[16,1024]{1,0:T(8,128)(2,1)} %bitcast.7, bf16[1024,1024]{1,0:T(8,128)(2,1)} %vw_hbm.1, bf16[192,1024]{1,0:T(8,128)(2,1)} %bitcast.6, bf16[64,1024]{1,0:T(8,128)(2,1)} %ow_hbm.1, bf16[1024,256]{1,0:T(8,128)(2,1)} %up_hbm.1, bf16[256,1024]{1,0:T(8,128)(2,1)} %dw_hbm.1, ...), custom_call_target="tpu_custom_call" | custom-call | tf_op jit(solution)/shard_map/pallas_call | solution.py:338
  80.8 1.3 %copy.10 = bf16[8,1024]{1,0:T(8,128)(2,1)} copy(bf16[8,1024]{1,0:T(8,128)(2,1)} %shard_map.82) | data formatting | bytes 32768
